TPU v7x, 128 devices: a whole 4x4x4 slice. The times are simulated.
128 devices in a mesh: ctx: 16 (over z, y_lo, core), ch: 8 (over y_hi, x).
Axes of the slice: x: 4, y: 4 (y_hi: 2, y_lo: 2; y = y_hi * 2 + y_lo), z: 4, core: 2. Of those that a mesh axis runs over, the one named last changes fastest.
Arguments:
- tokens: bfloat16 [2048, 8192], P('ctx', 'ch'), may hold values from -6 to 6
- w_in: bfloat16 [8192, 3, 4096], P('ctx', None, 'ch'), may hold values from -0.0625 to 0.0625
- short_filter: float32 [3, 3, 4096], P(None, None, 'ch'), may hold values from -3 to 3
- decay_rate: float32 [256, 16], P('ch'), may hold values from 0.00024414062 to 0.1
- residue: float32 [256, 16], P('ch'), may hold values from -1.5 to 1.5
- skip: float32 [4096], P('ch'), may hold values from -6 to 6
Outputs:
- block_out: bfloat16 [2048, 4096], P('ctx', 'ch')
All inputs are finite; a program needn't handle non-finite values.
Results may differ from a plain program's by a relative error of at most 0.011.
Values may be sent and summed in bfloat16 or wider, within the bound.
A program may use at most 128 MiB of HBM per device.

v0:
```python
import math
import jax
import jax.numpy as jnp
from jax import lax
from jax.sharding import PartitionSpec as P

GROUP = 16


def shifted(block, axis, distance):
    devices = range(lax.axis_size(axis))
    route = [(i - distance, i) for i in devices if i - distance in devices]
    return lax.ppermute(block, axis, route)


def short_mix(projected, short_filter_taps, block_len, local_width):
    rounded = lax.optimization_barrier(projected.astype(jnp.bfloat16))
    proj_rows = rounded.astype(jnp.float32).reshape(
        block_len + 2, short_filter_taps.shape[1], local_width
    )
    return (
        short_filter_taps[0] * proj_rows[2:]
        + short_filter_taps[1] * proj_rows[1:-1]
        + short_filter_taps[2] * proj_rows[:-2]
    )


def split_parts(weight_full):
    upper_triangle_part = weight_full.astype(jnp.bfloat16)
    lower_triangle_part = (weight_full - upper_triangle_part.astype(jnp.float32)).astype(
        jnp.bfloat16
    )
    return (upper_triangle_part, lower_triangle_part)


def decay_sum(weight_full, input_half_rows):
    upper_triangle_part, lower_triangle_part = split_parts(weight_full)
    first_sum = jnp.einsum(
        "lbu,lvu->lbv", upper_triangle_part, input_half_rows, preferred_element_type=jnp.float32
    )
    second_partial_sum = jnp.einsum(
        "lbu,lvu->lbv", lower_triangle_part, input_half_rows, preferred_element_type=jnp.float32
    )
    return first_sum + second_partial_sum


def local(tokens, w_in, short_filter, decay_rate, residue, skip):
    block_len = tokens.shape[0]
    local_width = w_in.shape[2]
    group_count = local_width // GROUP
    gathered = lax.all_gather(tokens, "ch", axis=1, tiled=True)
    previous = shifted(gathered[block_len - 2 :], "ctx", 1)
    extended = jnp.concatenate([previous, gathered], axis=0)
    shard_piece = lax.all_gather(w_in, "ctx", axis=0, tiled=True)
    flat_piece = shard_piece.reshape(shard_piece.shape[0], -1)
    proj_all = jnp.dot(extended, flat_piece, preferred_element_type=jnp.float32)
    short_mixed = short_mix(proj_all, short_filter, block_len, local_width)
    query_part = short_mixed[:, 0]
    key_part = short_mixed[:, 1]
    value_part = short_mixed[:, 2]
    gated_input = (key_part * value_part).astype(jnp.bfloat16)
    input_t = gated_input.T
    columns_t = input_t.reshape(group_count, GROUP, block_len)
    pole_weight = residue * jnp.sqrt(2.0 * decay_rate)
    positions = jnp.arange(block_len).astype(jnp.float32)
    near_filter = jnp.einsum(
        "gr,grl->gl",
        pole_weight,
        jnp.exp(-decay_rate[:, :, None] * positions[None, None, :]),
        precision=lax.Precision.HIGHEST,
    )
    padded_filter = jnp.concatenate(
        [
            jnp.zeros((group_count, block_len - 1), jnp.float32),
            near_filter,
            jnp.zeros((group_count, 1), jnp.float32),
        ],
        axis=1,
    )

    def near_one(item_pair):
        filter_row, tok_block = item_pair
        span_len = 2 * block_len - 1
        tiled_rows = jnp.tile(filter_row, block_len)[: block_len * span_len].reshape(
            block_len, span_len
        )
        toeplitz = tiled_rows[:, block_len - 1 :]
        upper_triangle_part, lower_triangle_part = split_parts(toeplitz)
        return jnp.dot(
            tok_block, upper_triangle_part, preferred_element_type=jnp.float32
        ) + jnp.dot(tok_block, lower_triangle_part, preferred_element_type=jnp.float32)

    near_field = lax.map(near_one, (padded_filter, columns_t), batch_size=2)
    my_start = lax.axis_index("ctx") * block_len
    empty_state = jnp.zeros((group_count, decay_rate.shape[1], GROUP), jnp.float32)
    shard_piece = lax.all_gather(input_t, "ctx", axis=1, tiled=True)
    piece_len = shard_piece.shape[1]
    sub_len = math.gcd(piece_len, block_len)

    def sub_step(turn_index, carried):
        part_cols = lax.dynamic_slice_in_dim(shard_piece, turn_index * sub_len, sub_len, 1)
        distance = (my_start - 1 - turn_index * sub_len - jnp.arange(sub_len)).astype(jnp.float32)
        decay_factor_weight = jnp.where(
            distance[None, None, :] >= 0.0,
            jnp.exp(-decay_rate[:, :, None] * jnp.maximum(distance, 0.0)[None, None, :]),
            0.0,
        )
        part_input = part_cols.reshape(group_count, GROUP, sub_len)
        return carried + decay_sum(decay_factor_weight, part_input)

    past_state = lax.fori_loop(0, piece_len // sub_len, sub_step, empty_state)
    far_weight = pole_weight[:, :, None] * jnp.exp(
        -decay_rate[:, :, None] * (positions + 1.0)[None, None, :]
    )
    distant_field_output = jnp.einsum(
        "grc,gri->gci", past_state, far_weight, precision=lax.Precision.HIGHEST
    )
    long_out = (near_field + distant_field_output).reshape(local_width, block_len).T
    return (query_part * (long_out + skip * gated_input.astype(jnp.float32))).astype(jnp.bfloat16)


def solution(mesh):
    return jax.shard_map(
        local,
        mesh=mesh,
        in_specs=(
            P("ctx", "ch"),
            P("ctx", None, "ch"),
            P(None, None, "ch"),
            P("ch", None),
            P("ch", None),
            P("ch"),
        ),
        out_specs=P("ctx", "ch"),
        check_vma=False,
    )
```

profile of v0, /device:TPU:1, one launch (start us, length us, event | category | flops | bytes accessed | tf_op | source)
XLA Modules:
  0.0 289.3 jit_solution(2068078018637368503)
XLA Ops:
  7.3 2.6 copy.16
  10.8 55.6 %all-gather.4.cloned.1.call-done = bf16[128,8192]{1,0:T(8,128)(2,1)} async-done(((bf16[128,1024]{1,0:T(8,128)(2,1)}), bf16[128,8192]{1,0:T(8,128)(2,1)}) %all-gather.4.cloned.1.call-update) | async-done | bytes 2097168 | tf_op jit(solution)/shard_map/all_gather | solution.py:51
  66.5 0.9 slice.60
  67.4 4.0 %collective-permute-start = (bf16[2,8192]{1,0:T(2,128)(2,1)S(1)}, bf16[2,8192]{1,0:T(2,128)(2,1)S(1)}, u32[]{:S(2)}, u32[]{:S(2)}) collective-permute-start(bf16[2,8192]{1,0:T(2,128)(2,1)S(1)} %slice.60), channel_id=1, source_target_pairs={{0,8},{8,16},{16,24},{24,32},{32,40},{40,48},{48,56},{56,64},{64,7... | collective-permute-start | bytes 98312 | tf_op jit(solution)/shard_map/ppermute | solution.py:13
  72.5 127.4 %all-gather.6.cloned.1.call-done = bf16[8192,3,512]{0,2,1:T(8,128)(2,1)} async-done(((bf16[512,3,512]{0,2,1:T(8,128)(2,1)}), bf16[8192,3,512]{0,2,1:T(8,128)(2,1)}) %all-gather.6.cloned.1.call-update) | async-done | bytes 25165840 | tf_op jit(solution)/shard_map/all_gather | solution.py:54
  199.9 13.7 %convolution_convert_fusion = bf16[130,1536]{1,0:T(8,128)(2,1)S(1)} fusion(bf16[8192,1536]{0,1:T(8,128)(2,1)} %bitcast.89, bf16[128,8192]{1,0:T(8,128)(2,1)} %all-gather.4.cloned.1.call-done, bf16[2,8192]{1,0:T(2,128)(2,1)S(1)} %collective-permute-done), kind=kOutput, calls=%fused_computation.34 | convolution fusion | flops 3276016640 | bytes 27695104 | tf_op jit(solution)/shard_map/dot_general | solution.py:56
  213.8 1.2 copy.19
  217.6 27.3 %while.26 = (s32[]{:T(128)}, f32[16,2,16,128]{3,2,1,0:T(8,128)}, bf16[16,2,16,128]{3,2,1,0:T(8,128)(2,1)S(1)}, f32[16,2,256]{2,1,0:T(2,128)S(1)}, s32[]{:T(128)}) while((s32[]{:T(128)}, f32[16,2,16,128]{3,2,1,0:T(8,128)}, bf16[16,2,16,128]{3,2,1,0:T(8,128)(2,1)S(1)}, f32[16,2,256]{2,1,0:T(2,128)S(1)}, s32[]{:T(128)}) %tuple.71), condition=%wide.region_1.2_spmd, body=%wide.region_0.1_spmd.sunk | while | flops 2232322 | bytes 2100301 | solution.py:93
  245.0 11.1 %all-gather.8.cloned.1.call-done = bf16[512,2048]{1,0:T(8,128)(2,1)} async-done(((bf16[512,128]{1,0:T(8,128)(2,1)}), bf16[512,2048]{1,0:T(8,128)(2,1)}) %all-gather.8.cloned.1.call-update) | async-done | bytes 2097168 | tf_op jit(solution)/shard_map/all_gather | solution.py:96
  256.1 25.0 %while.27 = (s32[]{:T(128)}, f32[32,16,16]{2,1,0:T(8,128)S(1)}, s32[]{:T(128)}, f32[32,16,1]{1,0,2:T(8,128)S(1)}, bf16[512,2048]{1,0:T(8,128)(2,1)}, /*index=5*/s32[]{:T(128)}, s32[]{:T(128)}, s32[]{:T(128)}, s32[]{:T(128)}) while((s32[]{:T(128)}, f32[32,16,16]{2,1,0:T(8,128)S(1)}, s32[]{:T(128)}, f32[32,16,1]{1,0,2:T(8,128)S(1)}, ...), condition=%wide.region_3.4_spmd.clone, body=%wide.region_2.3_spmd.clone.sunk | while | flops 4809480 | bytes 661557 | solution.py:111
  256.1 1.0 constant_dynamic-slice_fusion.2
  257.7 0.9 constant_dynamic-slice_fusion.2
  259.2 0.9 constant_dynamic-slice_fusion.2
  260.8 0.9 constant_dynamic-slice_fusion.2
  262.3 0.9 constant_dynamic-slice_fusion.2
  263.9 0.9 constant_dynamic-slice_fusion.2
  265.5 0.9 constant_dynamic-slice_fusion.2
  267.0 0.9 constant_dynamic-slice_fusion.2
  268.6 0.9 constant_dynamic-slice_fusion.2
  270.1 0.9 constant_dynamic-slice_fusion.2
  271.7 0.9 constant_dynamic-slice_fusion.2
  273.3 0.9 constant_dynamic-slice_fusion.2
  274.8 0.9 constant_dynamic-slice_fusion.2
  279.5 0.9 constant_dynamic-slice_fusion.2
  (222 shorter events, 45.1 us)
Async XLA Ops:
  6.5 59.9 %all-gather.4.cloned.1.call-start = ((), (), s32[]{:S(2)}) async-start(), calls=%async_computation | async-start | bytes 2359296 | tf_op jit(solution)/shard_map/all_gather | solution.py:51
  7.3 2.8 copy-start.2
  7.3 2.8 copy-start.4
  7.3 3.0 %copy-start.3 = (f32[3,3,512]{2,1,0:T(4,128)S(1)}, f32[3,3,512]{2,1,0:T(4,128)}, u32[]{:S(2)}) copy-start(f32[3,3,512]{2,1,0:T(4,128)} %param.12) | copy-start | bytes 55300
  7.3 192.6 %all-gather.6.cloned.1.call-start = ((), (), s32[]{:S(2)}) async-start(), calls=%async_computation.1 | async-start | bytes 26738688 | tf_op jit(solution)/shard_map/all_gather | solution.py:54
  10.0 246.1 %all-gather.8.cloned.1.call-start = ((), (), s32[]{:S(2)}) async-start(), calls=%async_computation.2 | async-start | bytes 2228224 | tf_op jit(solution)/shard_map/all_gather | solution.py:96
  67.4 5.1 %collective-permute-start = (bf16[2,8192]{1,0:T(2,128)(2,1)S(1)}, bf16[2,8192]{1,0:T(2,128)(2,1)S(1)}, u32[]{:S(2)}, u32[]{:S(2)}) collective-permute-start(bf16[2,8192]{1,0:T(2,128)(2,1)S(1)} %slice.60), channel_id=1, source_target_pairs={{0,8},{8,16},{16,24},{24,32},{32,40},{40,48},{48,56},{56,64},{64,7... | collective-permute-start | bytes 98312 | tf_op jit(solution)/shard_map/ppermute | solution.py:13
  215.0 1.1 copy-start
  256.1 25.0 %copy-start.1 = (f32[16,2,16,128]{3,2,1,0:T(8,128)S(1)}, f32[16,2,16,128]{3,2,1,0:T(8,128)}, u32[]{:S(2)}) copy-start(f32[16,2,16,128]{3,2,1,0:T(8,128)} %get-tuple-element.158) | copy-start | bytes 786436
  256.1 25.8 %copy-start.5 = (f32[512]{0:T(512)S(1)}, f32[512]{0:T(512)}, u32[]{:S(2)}) copy-start(f32[512]{0:T(512)} %param.15) | copy-start | bytes 6148
Sparse Core Ops, SparseCore 0:
  9.7 56.7 all-gather.3
  68.1 131.7 all-gather.5
  217.8 38.2 all-gather.7
where the time goes:
time: 290 us; the launch traced here: 289 us
  waiting for transfers between devices  196 us (68%)
  matrix products  40.5 us (14%)
  local copies, waits for them, and re-layouts  32.3 us (11%)
  between operations  13.3 us (5%)
  starting transfers between devices  4.13 us (1%)
    all_gather x1, waiting for transfers between devices, local(): shard_piece = lax.all_gather(w_in, 'ctx', axis=0, tiled=True)  127 us
    all_gather x1, waiting for transfers between devices, local(): gathered = lax.all_gather(tokens, 'ch', axis=1, tiled=True)  55.6 us
    dynamic_slice x16, local copies, waits for them, and re-layouts, sub_step(): lax.dynamic_slice_in_dim(shard_piece, turn_index * sub_len, sub_len, 1)  14.7 us
    dot_general x1, matrix products, local(): proj_all = jnp.dot(extended, flat_piece, preferred_element_type=jnp.float32)  13.7 us
    dot_general x16, matrix products, near_one(): jnp.dot(tok_block, lower_triangle_part, preferred_element_type=jnp.float32)  13.2 us
    all_gather x1, waiting for transfers between devices, local(): shard_piece = lax.all_gather(input_t, 'ctx', axis=1, tiled=True)  11.1 us
    reshape x16, local copies, waits for them, and re-layouts, near_one(): jnp.tile(filter_row, block_len)[:block_len * span_len]  6.48 us
  transfers between devices with their start and end apart: 4, of which 4 were waited for; matrix products, arithmetic and copies ran while one was open for 11% of the time, Pallas kernels for 0%

commit v1 on v0

--- a/solution.py
+++ b/solution.py
@@ -93,7 +93,15 @@
     near_field = lax.map(near_one, (padded_filter, columns_t), batch_size=2)
     my_start = lax.axis_index("ctx") * block_len
     empty_state = jnp.zeros((group_count, decay_rate.shape[1], GROUP), jnp.float32)
-    shard_piece = lax.all_gather(input_t, "ctx", axis=1, tiled=True)
+    shard_piece = jnp.concatenate(
+        jax.lax.all_to_all(
+            jnp.stack([input_t for _ in range(jax.lax.axis_size("ctx"))], axis=0),
+            axis_name="ctx",
+            split_axis=0,
+            concat_axis=0,
+        ),
+        axis=1,
+    )
     piece_len = shard_piece.shape[1]
     sub_len = math.gcd(piece_len, block_len)
 

time: 290 us -> 299 us (1.031)
  waiting for transfers between devices: 196 us -> 183 us
  matrix products: 40.5 us -> 51.2 us
  starting transfers between devices: 4.13 us -> 9.18 us
  local copies, waits for them, and re-layouts: 32.3 us -> 36.8 us
    dynamic_slice x16 -> x32, local copies, waits for them, and re-layouts: 14.7 us -> 2.14 us  [sub_step(): lax.dynamic_slice_in_dim(shard_piece, turn_index * sub_len, sub_len, 1)]
    while x32 -> x96, local copies, waits for them, and re-layouts: 3.62 us -> 15.5 us
    all_gather x1 -> x0, waiting for transfers between devices: 11.1 us -> none  [local(): shard_piece = lax.all_gather(input_t, 'ctx', axis=1, tiled=True)]
    dot_general x16, matrix products: 4.81 us -> 14.5 us  [decay_sum(): jnp.einsum('lbu,lvu->lbv', lower_triangle_part, input_half_rows, preferre...]
    all_to_all x0 -> x1, starting transfers between devices: none -> 5.09 us  [local(): jax.lax.all_to_all(jnp.stack([input_t for _ in range(jax.lax.axis_size('c...]
  transfers between devices with their start and end apart: 4 -> 4, of which waited for: 4 -> 2; matrix products, arithmetic and copies ran while one was open for 11% -> 11% of each run, Pallas kernels for 0% -> 0%
where the time goes in v1:
time: 299 us; the launch traced here: 298 us
  waiting for transfers between devices  183 us (61%)
  matrix products  51.2 us (17%)
  local copies, waits for them, and re-layouts  36.8 us (12%)
  between operations  13.6 us (5%)
  starting transfers between devices  9.18 us (3%)
    all_gather x1, waiting for transfers between devices, local(): shard_piece = lax.all_gather(w_in, 'ctx', axis=0, tiled=True)  127 us
    all_gather x1, waiting for transfers between devices, local(): gathered = lax.all_gather(tokens, 'ch', axis=1, tiled=True)  55.7 us
    while x96, local copies, waits for them, and re-layouts  15.5 us
    dot_general x16, matrix products, decay_sum(): jnp.einsum('lbu,lvu->lbv', lower_triangle_part, input_half_rows, preferre...  14.5 us
    dot_general x1, matrix products, local(): proj_all = jnp.dot(extended, flat_piece, preferred_element_type=jnp.float32)  13.7 us
    dot_general x16, matrix products, near_one(): jnp.dot(tok_block, lower_triangle_part, preferred_element_type=jnp.float32)  13.2 us
    reshape x16, local copies, waits for them, and re-layouts, near_one(): jnp.tile(filter_row, block_len)[:block_len * span_len]  6.48 us
  transfers between devices with their start and end apart: 4, of which 2 were waited for; matrix products, arithmetic and copies ran while one was open for 11% of the time, Pallas kernels for 0%

profile of v1, /device:TPU:1, one launch (start us, length us, event | category | flops | bytes accessed | tf_op | source)
XLA Modules:
  0.0 298.3 jit_solution(13597870589434384159)
XLA Ops:
  7.3 2.6 copy.32
  10.8 55.7 %all-gather.3.cloned.1.call-done = bf16[128,8192]{1,0:T(8,128)(2,1)} async-done(((bf16[128,1024]{1,0:T(8,128)(2,1)}), bf16[128,8192]{1,0:T(8,128)(2,1)}) %all-gather.3.cloned.1.call-update) | async-done | bytes 2097168 | tf_op jit(solution)/shard_map/all_gather | solution.py:51
  66.5 0.9 slice.60
  67.4 4.0 %collective-permute-start = (bf16[2,8192]{1,0:T(2,128)(2,1)S(1)}, bf16[2,8192]{1,0:T(2,128)(2,1)S(1)}, u32[]{:S(2)}, u32[]{:S(2)}) collective-permute-start(bf16[2,8192]{1,0:T(2,128)(2,1)S(1)} %slice.60), channel_id=1, source_target_pairs={{0,8},{8,16},{16,24},{24,32},{32,40},{40,48},{48,56},{56,64},{64,7... | collective-permute-start | bytes 98312 | tf_op jit(solution)/shard_map/ppermute | solution.py:13
  72.8 127.1 %all-gather.5.cloned.1.call-done = bf16[8192,3,512]{0,2,1:T(8,128)(2,1)} async-done(((bf16[512,3,512]{0,2,1:T(8,128)(2,1)}), bf16[8192,3,512]{0,2,1:T(8,128)(2,1)}) %all-gather.5.cloned.1.call-update) | async-done | bytes 25165840 | tf_op jit(solution)/shard_map/all_gather | solution.py:54
  199.9 13.7 %convolution_convert_fusion = bf16[130,1536]{1,0:T(8,128)(2,1)S(1)} fusion(bf16[8192,1536]{0,1:T(8,128)(2,1)} %bitcast.93, bf16[128,8192]{1,0:T(8,128)(2,1)} %all-gather.3.cloned.1.call-done, bf16[2,8192]{1,0:T(2,128)(2,1)S(1)} %collective-permute-done), kind=kOutput, calls=%fused_computation.34 | convolution fusion | flops 3276016640 | bytes 27695104 | tf_op jit(solution)/shard_map/dot_general | solution.py:56
  213.9 1.2 copy.35
  217.0 1.7 stack.2
  218.7 5.1 %all-to-all-start = ((bf16[16,512,128]{2,1,0:T(8,128)(2,1)}), bf16[16,512,128]{2,1,0:T(8,128)(2,1)}, u32[]{:S(2)}, u32[]{:S(2)}) async-start(bf16[16,512,128]{2,1,0:T(8,128)(2,1)} %stack.2), calls=%async_computation | async-start | bytes 4194304 | tf_op jit(solution)/shard_map/all_to_all | solution.py:97
  223.8 27.3 %while.26 = (s32[]{:T(128)}, f32[16,2,16,128]{3,2,1,0:T(8,128)}, bf16[16,2,16,128]{3,2,1,0:T(8,128)(2,1)S(1)}, f32[16,2,256]{2,1,0:T(2,128)S(1)}, s32[]{:T(128)}) while((s32[]{:T(128)}, f32[16,2,16,128]{3,2,1,0:T(8,128)}, bf16[16,2,16,128]{3,2,1,0:T(8,128)(2,1)S(1)}, f32[16,2,256]{2,1,0:T(2,128)S(1)}, s32[]{:T(128)}) %tuple.70), condition=%wide.region_1.2_spmd, body=%wide.region_0.1_spmd.sunk | while | flops 2232322 | bytes 2100301 | solution.py:93
  251.2 2.9 copy.37
  254.0 34.1 %while.27 = (s32[]{:T(128)}, f32[32,16,16]{2,1,0:T(8,128)S(1)}, s32[]{:T(128)}, f32[32,16,1]{1,0,2:T(8,128)S(1)}, bf16[512,2048]{0,1:T(8,128)(2,1)S(1)}, /*index=5*/s32[]{:T(128)}, s32[]{:T(128)}, s32[]{:T(128)}, s32[]{:T(128)}) while((s32[]{:T(128)}, f32[32,16,16]{2,1,0:T(8,128)S(1)}, s32[]{:T(128)}, f32[32,16,1]{1,0,2:T(8,128)S(1)}, ...), condition=%wide.region_3.4_spmd.clone, body=%wide.region_2.3_spmd.clone.sunk | while | flops 4809480 | bytes 926317 | solution.py:119
  255.2 0.9 fusion.65
  257.4 0.9 fusion.65
  259.5 0.9 fusion.65
  261.6 0.9 fusion.65
  263.8 0.9 fusion.65
  265.9 0.9 fusion.65
  268.0 0.9 fusion.65
  272.3 0.9 fusion.65
  278.7 0.9 fusion.65
  280.8 0.9 fusion.65
  285.1 0.9 fusion.65
  288.1 1.7 convolution_add_fusion.2
  (301 shorter events, 56.6 us)
Async XLA Ops:
  6.5 59.9 %all-gather.3.cloned.1.call-start = ((), (), s32[]{:S(2)}) async-start(), calls=%async_computation.1 | async-start | bytes 2359296 | tf_op jit(solution)/shard_map/all_gather | solution.py:51
  7.3 2.7 copy-start.2
  7.3 2.8 copy-start.6
  7.3 3.0 copy-start.3
  7.3 192.6 %all-gather.5.cloned.1.call-start = ((), (), s32[]{:S(2)}) async-start(), calls=%async_computation.2 | async-start | bytes 26738688 | tf_op jit(solution)/shard_map/all_gather | solution.py:54
  10.3 61.8 %copy-start.1 = (f32[32,16]{1,0:T(8,128)}, f32[32,16]{1,0:T(8,128)S(1)}, u32[]{:S(2)}) copy-start(f32[32,16]{1,0:T(8,128)S(1)} %get-tuple-element.212) | copy-start | bytes 6148
  67.4 5.3 %collective-permute-start = (bf16[2,8192]{1,0:T(2,128)(2,1)S(1)}, bf16[2,8192]{1,0:T(2,128)(2,1)S(1)}, u32[]{:S(2)}, u32[]{:S(2)}) collective-permute-start(bf16[2,8192]{1,0:T(2,128)(2,1)S(1)} %slice.60), channel_id=1, source_target_pairs={{0,8},{8,16},{16,24},{24,32},{32,40},{40,48},{48,56},{56,64},{64,7... | collective-permute-start | bytes 98312 | tf_op jit(solution)/shard_map/ppermute | solution.py:13
  215.0 1.1 copy-start
  218.7 32.4 %all-to-all-start = ((bf16[16,512,128]{2,1,0:T(8,128)(2,1)}), bf16[16,512,128]{2,1,0:T(8,128)(2,1)}, u32[]{:S(2)}, u32[]{:S(2)}) async-start(bf16[16,512,128]{2,1,0:T(8,128)(2,1)} %stack.2), calls=%async_computation | async-start | bytes 4194304 | tf_op jit(solution)/shard_map/all_to_all | solution.py:97
  254.7 0.5 copy-start.5
  256.9 0.5 copy-start.5
  259.0 0.5 copy-start.5
  261.1 0.5 copy-start.5
  263.2 0.5 copy-start.5
  265.4 0.5 copy-start.5
  267.5 0.5 copy-start.5
  269.6 0.5 copy-start.5
  271.8 0.5 copy-start.5
  273.9 0.5 copy-start.5
  276.0 0.5 copy-start.5
  278.2 0.5 copy-start.5
  280.3 0.5 copy-start.5
  282.4 0.5 copy-start.5
  284.6 0.5 copy-start.5
  (17 other events, 8.7 us)
Sparse Core Ops, SparseCore 0:
  9.7 56.7 all-gather.2
  68.1 131.6 all-gather.4
